TPU v7x, 512 devices: a whole 4x4x16 slice. The times are simulated.
512 devices in a mesh: docs: 64 (over x, z_lo, core), blk: 8 (over y, z_hi).
Axes of the slice: x: 4, y: 4, z: 16 (z_hi: 2, z_lo: 8; z = z_hi * 8 + z_lo), core: 2. Of those that a mesh axis runs over, the one named last changes fastest.
Arguments:
- group_rows: bfloat16 [8, 16384, 2048], P('blk', 'docs'), may hold values from -0.14941406 to 0.14941406
- group_owner: int32 [8, 16384, 1], P('blk', 'docs'), may hold values from 0 to 63; in each aligned block of 256 rows (0 to 255, 256 to 511, ..., all dimensions but the last counted through in order) at most 8 rows name the same one
- group_doc: int32 [8, 16384], P('blk', 'docs'), may hold values from 0 to 255
- doc_weight: float32 [8, 16384], P('blk', 'docs'), may hold values from 0.1 to 1
- queries: bfloat16 [256, 2048], P('blk'), may hold values from -6 to 6
- precond: bfloat16 [2048, 2048], P(None, 'docs'), may hold values from -0.125 to 0.125
Outputs:
- scores: float32 [256, 8, 16384], P(None, 'blk', 'docs')
Inputs may be any that keep to these rules, and one draw needn't show every extreme that they name: `group_owner`: within the rows of one device, at most 8 groups name the same owner, and some owner gets exactly 8.
All inputs are finite; a program needn't handle non-finite values.
Results may differ from a plain program's by a relative error of at most 0.006.
Values may be sent and summed in bfloat16 or wider, within the bound.
A program may use at most 64 MiB of HBM per device.

v0:
```python
import jax
import jax.numpy as jnp
from jax import lax
from jax.sharding import PartitionSpec as P


def against_docs(left, high_part, low_part, weight):
    dims = (((1,), (1,)), ((), ()))
    product = lax.dot_general(left, high_part, dims, preferred_element_type=jnp.float32)
    product = product + lax.dot_general(left, low_part, dims, preferred_element_type=jnp.float32)
    return product * weight[None, :]


def shards(group_rows, group_owner, group_doc, doc_weight, queries, precond):
    rows = group_rows[0]
    owner = group_owner[0, :, 0]
    doc_index = group_doc[0]
    peers = lax.axis_size("docs")
    count = rows.shape[0]
    width = rows.shape[1]
    capacity = 2 * count // peers
    peer_ids = jnp.arange(peers, dtype=jnp.int32)
    owner_table = (owner[:, None] == peer_ids[None, :]).astype(jnp.int32)
    earlier = jnp.cumsum(owner_table, axis=0) - owner_table
    slot = jnp.sum(earlier * owner_table, axis=1)
    send_ids = jnp.full((peers, capacity), -1, jnp.int32).at[owner, slot].set(doc_index)
    doc_count = doc_weight.shape[1]
    doc_ids = jnp.arange(doc_count, dtype=jnp.int32)
    weight = doc_weight[0]
    query_pre = jnp.dot(queries, precond, preferred_element_type=jnp.float32).astype(jnp.bfloat16)
    send_rows = jnp.zeros((peers, capacity, width), jnp.bfloat16).at[owner, slot].set(rows)
    got_rows, got_ids = (
        lax.all_to_all(send_rows, "docs", split_axis=0, concat_axis=0, tiled=True),
        lax.all_to_all(send_ids, "docs", split_axis=0, concat_axis=0, tiled=True),
    )
    got_rows = got_rows.reshape(peers * capacity, width)
    got_ids = got_ids.reshape(peers * capacity)
    member_table = (doc_ids[:, None] == got_ids[None, :]).astype(jnp.bfloat16)
    doc_print = jnp.dot(member_table, got_rows, preferred_element_type=jnp.float32)
    high_part = doc_print.astype(jnp.bfloat16)
    low_part = (doc_print - high_part.astype(jnp.float32)).astype(jnp.bfloat16)
    full_rows = lax.all_gather(query_pre, "docs", axis=1, tiled=True)
    scores = against_docs(
        lax.all_gather(full_rows, "blk", axis=0, tiled=True), high_part, low_part, weight
    )
    return scores[:, None, :]


def solution(mesh):
    return jax.shard_map(
        shards,
        mesh=mesh,
        in_specs=(
            P("blk", "docs", None),
            P("blk", "docs", None),
            P("blk", "docs"),
            P("blk", "docs"),
            P("blk", None),
            P(None, "docs"),
        ),
        out_specs=P(None, "blk", "docs"),
        check_vma=False,
    )
```

profile of v0, /device:TPU:2, one launch (start us, length us, event | category | flops | bytes accessed | tf_op | source)
XLA Modules:
  0.0 392.6 jit_solution(211520665865208457)
XLA Ops:
  6.5 0.7 fusion.11
  7.3 0.6 reduce-window.6
  7.9 0.2 slice_reduce_fusion
  8.1 0.8 fusion.10
  8.9 0.7 or_select_fusion
  9.6 21.2 %scatter_fusion = s32[64,8]{0,1:T(8,128)S(1)} fusion(s32[64,8]{0,1:T(8,128)S(1)} %broadcast_in_dim.6, s32[256]{0:T(256)S(1)} %bitcast.39, s32[256]{0:T(256)} %bitcast.45), kind=kCustom, calls=%fused_computation | custom fusion | bytes 5120 | tf_op jit(solution)/shard_map/scatter | solution.py:26
  30.8 0.7 copy.18
  31.5 16.1 %all-to-all-start = ((s32[64,1,8]{2,1,0:T(1,128)}), s32[64,1,8]{2,1,0:T(1,128)S(1)}, u32[]{:S(2)}, u32[]{:S(2)}) async-start(s32[64,1,8]{2,1,0:T(1,128)} %copy.18), calls=%async_computation | async-start | bytes 65536 | tf_op jit(solution)/shard_map/all_to_all | solution.py:34
  47.6 1.6 broadcast_in_dim.7
  49.2 44.4 %scatter_fusion.1 = bf16[64,8,2048]{2,1,0:T(8,128)(2,1)} fusion(bf16[64,8,2048]{2,1,0:T(8,128)(2,1)} %broadcast_in_dim.7, s32[256]{0:T(256)S(1)} %bitcast.40, bf16[256,2048]{1,0:T(8,128)(2,1)S(1)} %bitcast.41), kind=kCustom, calls=%fused_computation.1 | custom fusion | bytes 3147776 | tf_op jit(solution)/shard_map/scatter | solution.py:31
  93.6 13.4 %all-to-all-start.1 = ((bf16[64,8,2048]{2,1,0:T(8,128)(2,1)}), bf16[64,8,2048]{2,1,0:T(8,128)(2,1)}, u32[]{:S(2)}, u32[]{:S(2)}) async-start(bf16[64,8,2048]{2,1,0:T(8,128)(2,1)} %scatter_fusion.1), calls=%async_computation.1 | async-start | bytes 4194304 | tf_op jit(solution)/shard_map/all_to_all | solution.py:33
  107.0 0.0 all-gather.2.cloned.1.call-start
  107.0 0.2 convolution_convert_fusion
  107.2 0.1 copy.15
  107.3 181.2 %all_gather.6 = bf16[32,2048]{0,1:T(8,128)(2,1)S(1)} all-gather(bf16[32,32]{0,1:T(8,128)(2,1)S(1)} %copy.15), channel_id=1, replica_groups=mesh['docs'=64,'blk'=8] {'docs'}, dimensions={1}, use_global_device_ids=true | all-gather | bytes 133120 | tf_op jit(solution)/shard_map/all_gather | solution.py:42
  288.5 0.8 copy.16
  289.4 0.5 broadcast.101
  289.9 0.7 reduce.5
  290.6 0.1 eq.49
  290.7 2.3 fusion
  293.1 89.4 %all-gather.2.cloned.1.call-done = bf16[256,2048]{1,0:T(8,128)(2,1)} async-done(((bf16[32,2048]{1,0:T(8,128)(2,1)}), bf16[256,2048]{1,0:T(8,128)(2,1)}) %all-gather.2.cloned.1.call-update) | async-done | bytes 1048592 | tf_op jit(solution)/shard_map/all_gather | solution.py:44
  382.5 1.8 fusion.5
  384.3 0.5 fusion.3
  384.8 1.0 copy.19
  (16 shorter events, 0.1 us)
Async XLA Ops:
  6.5 100.5 %copy-start = (bf16[32,2048]{1,0:T(8,128)(2,1)S(1)}, bf16[32,2048]{1,0:T(8,128)(2,1)}, u32[]{:S(2)}) copy-start(bf16[32,2048]{1,0:T(8,128)(2,1)} %param.10) | copy-start | bytes 393220
  9.6 39.6 %copy-start.2 = (bf16[1,256,2048]{2,1,0:T(8,128)(2,1)S(1)}, bf16[1,256,2048]{2,1,0:T(8,128)(2,1)}, u32[]{:S(2)}) copy-start(bf16[1,256,2048]{2,1,0:T(8,128)(2,1)} %param.6) | copy-start | bytes 3145732
  31.5 62.1 %all-to-all-start = ((s32[64,1,8]{2,1,0:T(1,128)}), s32[64,1,8]{2,1,0:T(1,128)S(1)}, u32[]{:S(2)}, u32[]{:S(2)}) async-start(s32[64,1,8]{2,1,0:T(1,128)} %copy.18), calls=%async_computation | async-start | bytes 65536 | tf_op jit(solution)/shard_map/all_to_all | solution.py:34
  93.6 13.4 %copy-start.3 = (bf16[2048,32]{0,1:T(8,128)(2,1)S(1)}, bf16[2048,32]{0,1:T(8,128)(2,1)}, u32[]{:S(2)}) copy-start(bf16[2048,32]{0,1:T(8,128)(2,1)} %param.11) | copy-start | bytes 393220
  93.6 197.1 %all-to-all-start.1 = ((bf16[64,8,2048]{2,1,0:T(8,128)(2,1)}), bf16[64,8,2048]{2,1,0:T(8,128)(2,1)}, u32[]{:S(2)}, u32[]{:S(2)}) async-start(bf16[64,8,2048]{2,1,0:T(8,128)(2,1)} %scatter_fusion.1), calls=%async_computation.1 | async-start | bytes 4194304 | tf_op jit(solution)/shard_map/all_to_all | solution.py:33
  107.0 275.5 %all-gather.2.cloned.1.call-start = ((), (), s32[]{:S(2)}) async-start(), calls=%async_computation.2 | async-start | bytes 1179648 | tf_op jit(solution)/shard_map/all_gather | solution.py:44
  293.1 91.2 %copy-start.4 = (f32[1,256]{1,0:T(1,128)S(1)}, f32[1,256]{1,0:T(1,128)}, u32[]{:S(2)}) copy-start(f32[1,256]{1,0:T(1,128)} %param.9) | copy-start | bytes 3076
  382.5 1.8 copy-start.1
Sparse Core Ops, SparseCore 0:
  289.5 92.9 all-gather.1
where the time goes:
time: 395 us; the launch traced here: 393 us
  blocking collectives  181 us (46%)
  waiting for transfers between devices  89.4 us (23%)
  local copies, waits for them, and re-layouts  70.6 us (18%)
  starting transfers between devices  29.5 us (7%)
  between operations  13.5 us (3%)
  matrix products  4.72 us (1%)
    all_gather x1, blocking collectives, shards(): full_rows = lax.all_gather(query_pre, 'docs', axis=1, tiled=True)  181 us
    all_gather x1, waiting for transfers between devices, shards(): lax.all_gather(full_rows, 'blk', axis=0, tiled=True)  89.4 us
    scatter x1, local copies, waits for them, and re-layouts, shards(): jnp.zeros((peers, capacity, width), jnp.bfloat16).at[owner, slot].set(rows)  44.4 us
    scatter x1, local copies, waits for them, and re-layouts, shards(): jnp.full((peers, capacity), -1, jnp.int32).at[owner, slot].set(doc_index)  21.2 us
    all_to_all x1, starting transfers between devices, shards(): lax.all_to_all(send_ids, 'docs', split_axis=0, concat_axis=0, tiled=True)  16.1 us
    all_to_all x1, starting transfers between devices, shards(): lax.all_to_all(send_rows, 'docs', split_axis=0, concat_axis=0, tiled=True)  13.4 us
  transfers between devices with their start and end apart: 3, of which 1 were waited for; matrix products, arithmetic and copies ran while one was open for 13% of the time, Pallas kernels for 0%

commit v1 on v0

--- a/solution.py
+++ b/solution.py
@@ -2,6 +2,11 @@
 import jax.numpy as jnp
 from jax import lax
 from jax.sharding import PartitionSpec as P
+
+
+def _tell_trees(row_axis, pos_dim, mat):
+    local_now = lax.all_to_all(jnp.stack(lax.axis_size(row_axis) * [mat], axis=0), row_axis, 0, 0)
+    return jnp.concatenate(local_now, axis=pos_dim)
 
 
 def against_docs(left, high_part, low_part, weight):
@@ -39,7 +44,7 @@
     doc_print = jnp.dot(member_table, got_rows, preferred_element_type=jnp.float32)
     high_part = doc_print.astype(jnp.bfloat16)
     low_part = (doc_print - high_part.astype(jnp.float32)).astype(jnp.bfloat16)
-    full_rows = lax.all_gather(query_pre, "docs", axis=1, tiled=True)
+    full_rows = _tell_trees("docs", 1, query_pre)
     scores = against_docs(
         lax.all_gather(full_rows, "blk", axis=0, tiled=True), high_part, low_part, weight
     )

time: 395 us -> 263 us (0.67)
  the two profiles are of different devices: /device:TPU:2 before, /device:TPU:1 now
where the time goes in v1:
time: 263 us; the launch traced here: 261 us
  waiting for transfers between devices  132 us (50%)
  local copies, waits for them, and re-layouts  72.7 us (28%)
  starting transfers between devices  35 us (13%)
  between operations  13.6 us (5%)
  matrix products  4.72 us (2%)
  other arithmetic  3.56 us (1%)
    all_to_all x1, waiting for transfers between devices, shards(): lax.all_to_all(send_rows, 'docs', split_axis=0, concat_axis=0, tiled=True)  121 us
    scatter x1, local copies, waits for them, and re-layouts, shards(): jnp.zeros((peers, capacity, width), jnp.bfloat16).at[owner, slot].set(rows)  44.5 us
    scatter x1, local copies, waits for them, and re-layouts, shards(): jnp.full((peers, capacity), -1, jnp.int32).at[owner, slot].set(doc_index)  21.2 us
    all_to_all x1, starting transfers between devices, shards(): lax.all_to_all(send_ids, 'docs', split_axis=0, concat_axis=0, tiled=True)  17 us
    all_to_all x1, starting transfers between devices, shards(): lax.all_to_all(send_rows, 'docs', split_axis=0, concat_axis=0, tiled=True)  13.2 us
    all_to_all x1, waiting for transfers between devices, shards(): lax.all_to_all(send_ids, 'docs', split_axis=0, concat_axis=0, tiled=True)  10.9 us
  transfers between devices with their start and end apart: 4, of which 2 were waited for; matrix products, arithmetic and copies ran while one was open for 20% of the time, Pallas kernels for 0%

profile of v1, /device:TPU:1, one launch (start us, length us, event | category | flops | bytes accessed | tf_op | source)
XLA Modules:
  0.0 261.3 jit_solution(16710313332681598361)
XLA Ops:
  6.5 0.7 fusion.11
  7.3 0.6 reduce-window.6
  7.9 0.2 slice_reduce_fusion
  8.1 0.8 fusion.10
  8.9 0.7 or_select_fusion
  9.6 21.2 %scatter_fusion = s32[64,8]{0,1:T(8,128)S(1)} fusion(s32[64,8]{0,1:T(8,128)S(1)} %broadcast_in_dim.6, s32[256]{0:T(256)S(1)} %bitcast.40, s32[256]{0:T(256)} %bitcast.47), kind=kCustom, calls=%fused_computation | custom fusion | bytes 5120 | tf_op jit(solution)/shard_map/scatter | solution.py:31
  30.8 0.7 copy.13
  31.5 17.0 %all-to-all-start.1 = ((s32[64,1,8]{2,1,0:T(1,128)}), s32[64,1,8]{2,1,0:T(1,128)S(1)}, u32[]{:S(2)}, u32[]{:S(2)}) async-start(s32[64,1,8]{2,1,0:T(1,128)} %copy.13), calls=%async_computation.1 | async-start | bytes 65536 | tf_op jit(solution)/shard_map/all_to_all | solution.py:39
  48.9 1.1 reshape.99
  49.9 10.9 %all-to-all-done.1 = s32[64,1,8]{2,1,0:T(1,128)S(1)} async-done(((s32[64,1,8]{2,1,0:T(1,128)}), s32[64,1,8]{2,1,0:T(1,128)S(1)}, u32[]{:S(2)}, u32[]{:S(2)}) %all-to-all-start.1) | async-done | bytes 2080 | tf_op jit(solution)/shard_map/all_to_all | solution.py:39
  60.8 4.7 %all-to-all-start = ((bf16[64,2,512]{2,1,0:T(2,128)(2,1)}), bf16[64,2,512]{2,1,0:T(2,128)(2,1)S(1)}, u32[]{:S(2)}, u32[]{:S(2)}) async-start(bf16[64,2,512]{2,1,0:T(2,128)(2,1)} %reshape.99), calls=%async_computation | async-start | bytes 262144 | tf_op jit(solution)/shard_map/all_to_all | solution.py:8
  65.5 1.6 broadcast_in_dim.7
  67.1 44.5 %scatter_fusion.1 = bf16[64,8,2048]{2,1,0:T(8,128)(2,1)} fusion(bf16[64,8,2048]{2,1,0:T(8,128)(2,1)} %broadcast_in_dim.7, s32[256]{0:T(256)S(1)} %bitcast.41, bf16[256,2048]{1,0:T(8,128)(2,1)S(1)} %bitcast.43), kind=kCustom, calls=%fused_computation.1 | custom fusion | bytes 3147776 | tf_op jit(solution)/shard_map/scatter | solution.py:36
  111.6 13.2 %all-to-all-start.2 = ((bf16[64,8,2048]{2,1,0:T(8,128)(2,1)}), bf16[64,8,2048]{2,1,0:T(8,128)(2,1)}, u32[]{:S(2)}, u32[]{:S(2)}) async-start(bf16[64,8,2048]{2,1,0:T(8,128)(2,1)} %scatter_fusion.1), calls=%async_computation.2 | async-start | bytes 4194304 | tf_op jit(solution)/shard_map/all_to_all | solution.py:38
  124.9 0.3 reshape.100
  125.2 0.2 copy.11
  125.4 1.2 reshape.74
  126.6 0.5 broadcast.103
  127.2 0.7 reduce.5
  128.0 120.9 %all-to-all-done.2 = bf16[64,8,2048]{2,1,0:T(8,128)(2,1)} async-done(((bf16[64,8,2048]{2,1,0:T(8,128)(2,1)}), bf16[64,8,2048]{2,1,0:T(8,128)(2,1)}, u32[]{:S(2)}, u32[]{:S(2)}) %all-to-all-start.2) | async-done | bytes 2097184 | tf_op jit(solution)/shard_map/all_to_all | solution.py:38
  248.8 2.3 fusion
  251.2 1.8 fusion.5
  253.0 0.5 fusion.3
  253.5 1.0 copy.14
  (20 shorter events, 0.5 us)
Async XLA Ops:
  6.5 42.1 %copy-start = (bf16[32,2048]{1,0:T(8,128)(2,1)S(1)}, bf16[32,2048]{1,0:T(8,128)(2,1)}, u32[]{:S(2)}) copy-start(bf16[32,2048]{1,0:T(8,128)(2,1)} %param.10) | copy-start | bytes 393220
  6.5 42.1 %copy-start.3 = (bf16[2048,32]{0,1:T(8,128)(2,1)S(1)}, bf16[2048,32]{0,1:T(8,128)(2,1)}, u32[]{:S(2)}) copy-start(bf16[2048,32]{0,1:T(8,128)(2,1)} %param.11) | copy-start | bytes 393220
  30.8 36.3 %copy-start.2 = (bf16[1,256,2048]{2,1,0:T(8,128)(2,1)S(1)}, bf16[1,256,2048]{2,1,0:T(8,128)(2,1)}, u32[]{:S(2)}) copy-start(bf16[1,256,2048]{2,1,0:T(8,128)(2,1)} %param.6) | copy-start | bytes 3145732
  31.5 29.3 %all-to-all-start.1 = ((s32[64,1,8]{2,1,0:T(1,128)}), s32[64,1,8]{2,1,0:T(1,128)S(1)}, u32[]{:S(2)}, u32[]{:S(2)}) async-start(s32[64,1,8]{2,1,0:T(1,128)} %copy.13), calls=%async_computation.1 | async-start | bytes 65536 | tf_op jit(solution)/shard_map/all_to_all | solution.py:39
  60.8 50.8 %all-to-all-start = ((bf16[64,2,512]{2,1,0:T(2,128)(2,1)}), bf16[64,2,512]{2,1,0:T(2,128)(2,1)S(1)}, u32[]{:S(2)}, u32[]{:S(2)}) async-start(bf16[64,2,512]{2,1,0:T(2,128)(2,1)} %reshape.99), calls=%async_computation | async-start | bytes 262144 | tf_op jit(solution)/shard_map/all_to_all | solution.py:8
  111.6 137.2 %all-to-all-start.2 = ((bf16[64,8,2048]{2,1,0:T(8,128)(2,1)}), bf16[64,8,2048]{2,1,0:T(8,128)(2,1)}, u32[]{:S(2)}, u32[]{:S(2)}) async-start(bf16[64,8,2048]{2,1,0:T(8,128)(2,1)} %scatter_fusion.1), calls=%async_computation.2 | async-start | bytes 4194304 | tf_op jit(solution)/shard_map/all_to_all | solution.py:38
  124.9 126.3 %all-gather.2.cloned.1.call-start = ((), (), s32[]{:S(2)}) async-start(), calls=%async_computation.3 | async-start | bytes 1179648 | tf_op jit(solution)/shard_map/all_gather | solution.py:49
  251.1 1.8 copy-start.4
  251.2 1.8 copy-start.1
Sparse Core Ops, SparseCore 0:
  128.9 85.7 all-gather.1
